TPU v7x, 256 devices: a whole 4x4x8 slice. The times are simulated.
256 devices in a mesh: beam: 32 (over z_lo, x, core), tm: 8 (over z_hi, y).
Axes of the slice: x: 4, y: 4, z: 8 (z_hi: 2, z_lo: 4; z = z_hi * 4 + z_lo), core: 2. Of those that a mesh axis runs over, the one named last changes fastest.
Arguments:
- spectra: bfloat16 [1024, 128, 2, 2048], P('beam', 'tm'), may hold values from -6 to 6
- steering: bfloat16 [32, 2, 512, 1024], P('beam'), may hold values from -0.125 to 0.125
- templates: bfloat16 [256, 8, 2048], P(None, None, 'beam'), may hold values from -0.046875 to 0.046875
- tmpl_length: int32 [256], replicated, may hold values from 1 to 8
- band_start: int32 [256], replicated, may hold values from 0 to 1023
- band_width: int32 [256], replicated, may hold values from 256 to 1024
Outputs:
- scores: float32 [512, 128, 256], P('beam', 'tm')
Inputs may be any that keep to these rules, and one draw needn't show every extreme that they name: `tmpl_length`: lengths of templates in frames. band_start + band_width <= 2048.
All inputs are finite; a program needn't handle non-finite values.
Results may differ from a plain program's by a relative error of at most 0.0029.
Values may be sent and summed in bfloat16 or wider, within the bound.
A program may use at most 128 MiB of HBM per device.

v0:
```python
import jax
import jax.numpy as jnp
from jax import lax
from jax.sharding import PartitionSpec as P


def from_behind(block, axis, distance):
    devices = range(lax.axis_size(axis))
    route = [(i - distance, i) for i in devices if i - distance in devices]
    return lax.ppermute(block, axis, route)


def masked_templates(templates, tmpl_length, band_start, band_width):
    lag_count = templates.shape[1]
    bin_count = templates.shape[2]
    lag_index = jnp.arange(lag_count, dtype=jnp.int32)
    bin_index = jnp.arange(bin_count, dtype=jnp.int32)
    lag_keep = lag_index[None, :, None] < tmpl_length[:, None, None]
    band_end = band_start + band_width
    band_keep = (bin_index[None, None, :] >= band_start[:, None, None]) & (
        bin_index[None, None, :] < band_end[:, None, None]
    )
    return jnp.where(lag_keep & band_keep, templates, jnp.zeros_like(templates))


def correlate(extended, weights, frames):
    lag_count = weights.shape[1]
    total = jnp.einsum(
        "btk,mk->btm",
        extended[:, 0:frames, :],
        weights[:, 0, :],
        preferred_element_type=jnp.float32,
    )
    for offset in range(1, lag_count):
        total = total + jnp.einsum(
            "btk,mk->btm",
            extended[:, offset : offset + frames, :],
            weights[:, offset, :],
            preferred_element_type=jnp.float32,
        )
    return total


def per_device(spectra, steering, templates, tmpl_length, band_start, band_width):
    beam_count = lax.axis_size("beam")
    local_channels = spectra.shape[0]
    frames = spectra.shape[1]
    bin_total = spectra.shape[3]
    local_bins = bin_total // beam_count
    local_subbands = steering.shape[0]
    sub_width = local_bins // local_subbands
    subband_total = bin_total // sub_width
    regrouped = spectra.reshape(local_channels, frames, 2, subband_total, sub_width)
    regrouped = jnp.transpose(regrouped, (3, 0, 1, 2, 4)).reshape(
        subband_total, local_channels, frames, 2 * sub_width
    )
    block = lax.all_to_all(regrouped, "beam", split_axis=0, concat_axis=1, tiled=True)
    channels = block.shape[1]
    frame_part = block.shape[2]
    flat = block[0].reshape(channels, frame_part * 2 * sub_width)
    from_real = jnp.dot(steering[0, 0], flat, preferred_element_type=jnp.float32).reshape(
        -1, frame_part, 2, sub_width
    )
    from_imag = jnp.dot(steering[0, 1], flat, preferred_element_type=jnp.float32).reshape(
        -1, frame_part, 2, sub_width
    )
    beam_real = from_real[:, :, 0] - from_imag[:, :, 1]
    beam_imag = from_real[:, :, 1] + from_imag[:, :, 0]
    pieces = (beam_real * beam_real + beam_imag * beam_imag).astype(jnp.bfloat16)
    lag_count = templates.shape[1]
    next_rim = from_behind(pieces[:, : lag_count - 1, :], "tm", -1)
    extended = jnp.concatenate([pieces, next_rim], axis=1)
    owned = lax.all_to_all(extended, "beam", split_axis=0, concat_axis=2, tiled=True)
    weights = masked_templates(
        lax.all_gather(templates, "beam", axis=2, tiled=True), tmpl_length, band_start, band_width
    )
    return correlate(owned, weights, frames)


def solution(mesh):
    return jax.shard_map(
        per_device,
        mesh=mesh,
        in_specs=(
            P("beam", "tm", None, None),
            P("beam", None, None, None),
            P(None, None, "beam"),
            P(),
            P(),
            P(),
        ),
        out_specs=P("beam", "tm", None),
        check_vma=False,
    )
```

profile of v0, /device:TPU:57, one launch (start us, length us, event | category | flops | bytes accessed | tf_op | source)
XLA Modules:
  0.0 304.0 jit_solution(14706472602838422066)
XLA Ops:
  6.5 1.8 copy.28
  8.4 14.2 %reshape.89 = bf16[32,16,2,32,64]{4,3,2,1,0:T(8,128)(2,1)} reshape(bf16[32,16,2,2048]{3,2,1,0:T(2,128)(2,1)} %param.6) | data formatting | bytes 8388608 | tf_op jit(solution)/shard_map/reshape | solution.py:53
  22.6 13.2 %copy.45 = bf16[32,16,2,32,64]{4,2,1,0,3:T(2,128)(2,1)} copy(bf16[32,16,2,32,64]{4,3,2,1,0:T(8,128)(2,1)} %reshape.89) | data formatting | bytes 8388608 | tf_op jit(solution)/shard_map/reshape | solution.py:53
  35.8 14.2 %reshape.90 = bf16[32,32,16,128]{3,2,1,0:T(8,128)(2,1)} reshape(bf16[32,32,16,2,64]{4,3,2,1,0:T(2,128)(2,1)} %bitcast.67) | data formatting | bytes 8388608 | tf_op jit(solution)/shard_map/reshape | solution.py:54
  50.0 111.1 %all_to_all.27 = bf16[32,32,16,128]{3,2,1,0:T(8,128)(2,1)S(1)} all-to-all(bf16[32,32,16,128]{3,2,1,0:T(8,128)(2,1)} %reshape.90), channel_id=1, replica_groups=mesh['beam'=32,'tm'=8] {'beam'}, dimensions={0} | all-to-all | bytes 8388608 | tf_op jit(solution)/shard_map/all_to_all | solution.py:57
  161.0 4.1 %copy.46 = bf16[128,8,16,128]{3,1,2,0:T(8,128)(2,1)} copy(bf16[128,8,16,128]{3,2,1,0:T(8,128)(2,1)S(1)} %bitcast.68) | data formatting | bytes 8388608
  165.1 6.5 %copy.23 = bf16[2048,1024]{1,0:T(8,128)(2,1)} copy(bf16[2048,1024]{0,1:T(8,128)(2,1)} %bitcast.69) | data formatting | bytes 8388608 | tf_op jit(solution)/shard_map/dot_general | solution.py:61
  171.7 4.8 %fusion.14 = f32[512,16,2,64]{0,3,2,1:T(8,128)S(1)} fusion(bf16[16,2,64,1024]{3,2,1,0:T(8,128)(2,1)} %bitcast.71, bf16[1,2,512,1024]{3,2,1,0:T(8,128)(2,1)S(1)} %copy-done.5), kind=kOutput, calls=%fused_computation.37 | convolution fusion | flops 2147483648 | bytes 9437184 | tf_op jit(solution)/shard_map/dot_general | solution.py:64
  176.4 2.5 fusion.16
  179.0 1.1 fusion.20
  180.1 2.5 collective-permute-start
  182.6 26.0 %collective-permute-done = bf16[512,7,64]{0,2,1:T(8,128)(2,1)S(1)} collective-permute-done((bf16[512,7,64]{0,2,1:T(8,128)(2,1)S(1)}, bf16[512,7,64]{0,2,1:T(8,128)(2,1)S(1)}, u32[]{:S(2)}, u32[]{:S(2)}) %collective-permute-start) | collective-permute-done | bytes 458784 | tf_op jit(solution)/shard_map/ppermute | solution.py:10
  208.6 1.3 pad_maximum_fusion
  209.9 3.9 %copy.24 = bf16[512,23,64]{2,1,0:T(8,128)(2,1)S(1)} copy(bf16[512,23,64]{0,2,1:T(8,128)(2,1)} %pad_maximum_fusion) | data formatting | bytes 3014656 | tf_op jit(solution)/shard_map/concatenate | solution.py:72
  213.8 3.1 %reshape.102 = bf16[32,2,11776]{2,1,0:T(2,128)(2,1)} reshape(bf16[512,23,64]{2,1,0:T(8,128)(2,1)S(1)} %copy.24) | data formatting | bytes 3014656
  217.0 7.1 %all-to-all-start.1 = ((bf16[32,2,11776]{2,1,0:T(2,128)(2,1)}), bf16[32,2,11776]{2,1,0:T(2,128)(2,1)}, u32[]{:S(2)}, u32[]{:S(2)}) async-start(bf16[32,2,11776]{2,1,0:T(2,128)(2,1)} %reshape.102), calls=%async_computation.1 | async-start | bytes 3014656 | tf_op jit(solution)/shard_map/all_to_all | solution.py:73
  224.1 1.6 fusion.4
  225.7 34.9 %all-to-all-done.1 = bf16[32,2,11776]{2,1,0:T(2,128)(2,1)} async-done(((bf16[32,2,11776]{2,1,0:T(2,128)(2,1)}), bf16[32,2,11776]{2,1,0:T(2,128)(2,1)}, u32[]{:S(2)}, u32[]{:S(2)}) %all-to-all-start.1) | async-done | bytes 1507360 | tf_op jit(solution)/shard_map/all_to_all | solution.py:73
  260.6 5.5 %reshape.103 = bf16[512,23,64]{2,1,0:T(8,128)(2,1)S(1)} reshape(bf16[32,2,11776]{2,1,0:T(2,128)(2,1)} %all-to-all-done.1) | data formatting | bytes 3014656
  266.2 3.7 %copy.40 = bf16[16,23,32,64]{3,2,1,0:T(8,128)(2,1)} copy(bf16[16,23,32,64]{3,1,0,2:T(8,128)(2,1)S(1)} %bitcast.70) | data formatting | bytes 3014656 | tf_op jit(solution)/shard_map/all_to_all | solution.py:73
  269.9 4.4 %reshape.101 = bf16[16,23,2048]{2,1,0:T(8,128)(2,1)S(1)} reshape(bf16[16,23,32,64]{3,2,1,0:T(8,128)(2,1)} %copy.40) | data formatting | bytes 3014656 | tf_op jit(solution)/shard_map/all_to_all | solution.py:73
  274.3 12.6 %copy.29 = bf16[256,8,2048]{2,0,1:T(8,128)(2,1)} copy(bf16[256,8,2048]{0,1,2:T(8,128)(2,1)} %all-gather.2.cloned.1.call-done) | data formatting | bytes 16777216 | tf_op jit(solution)/shard_map/all_gather | solution.py:75
  287.0 5.5 %and_select_fusion = bf16[256,8,2048]{2,0,1:T(8,128)(2,1)S(1)} fusion(bf16[256,8,2048]{2,0,1:T(8,128)(2,1)} %copy.29, pred[256,2048]{1,0:T(8,128)(4,1)S(1)} %copy-done.1, pred[256,8]{0,1:T(8,128)(4,1)S(1)} %iota_compare_fusion.2), kind=kLoop, calls=%fused_computation | loop fusion | flops 8388608 | bytes 17303552 | tf_op jit(solution)/shard_map/jit(_where)/select_n | solution.py:23
  296.0 1.2 convolution_add_fusion
  (25 shorter events, 3.6 us)
Async XLA Ops:
  6.5 267.8 %all-gather.2.cloned.1.call-start = ((), (), s32[]{:S(2)}) async-start(), calls=%async_computation.2 | async-start | bytes 8650752 | tf_op jit(solution)/shard_map/all_gather | solution.py:75
  165.1 6.5 %copy-start.5 = (bf16[1,2,512,1024]{3,2,1,0:T(8,128)(2,1)S(1)}, bf16[1,2,512,1024]{3,2,1,0:T(8,128)(2,1)}, u32[]{:S(2)}) copy-start(bf16[1,2,512,1024]{3,2,1,0:T(8,128)(2,1)} %param.7) | copy-start | bytes 6291460
  171.7 4.8 %copy-start = (bf16[2048,1024]{1,0:T(8,128)(2,1)S(1)}, bf16[2048,1024]{1,0:T(8,128)(2,1)}, u32[]{:S(2)}) copy-start(bf16[2048,1024]{1,0:T(8,128)(2,1)} %copy.23) | copy-start | bytes 12582916
  180.1 28.5 %collective-permute-start = (bf16[512,7,64]{0,2,1:T(8,128)(2,1)S(1)}, bf16[512,7,64]{0,2,1:T(8,128)(2,1)S(1)}, u32[]{:S(2)}, u32[]{:S(2)}) collective-permute-start(bf16[512,7,64]{0,2,1:T(8,128)(2,1)S(1)} %slice.96), channel_id=1, source_target_pairs={{1,0},{2,1},{3,2},{4,3},{5,4},{6,5},{7,6},{9,8},{10,9},{11,10},{12... | collective-permute-start | bytes 1376264 | tf_op jit(solution)/shard_map/ppermute | solution.py:10
  213.8 10.3 %copy-start.2 = (s32[256]{0:T(256)S(1)}, s32[256]{0:T(256)}, u32[]{:S(2)}) copy-start(s32[256]{0:T(256)} %param.10) | copy-start | bytes 3076
  213.8 10.3 %copy-start.3 = (s32[256]{0:T(256)S(1)}, s32[256]{0:T(256)}, u32[]{:S(2)}) copy-start(s32[256]{0:T(256)} %param.11) | copy-start | bytes 3076
  213.8 10.3 %copy-start.4 = (s32[256]{0:T(256)S(1)}, s32[256]{0:T(256)}, u32[]{:S(2)}) copy-start(s32[256]{0:T(256)} %param.9) | copy-start | bytes 3076
  217.0 43.6 %all-to-all-start.1 = ((bf16[32,2,11776]{2,1,0:T(2,128)(2,1)}), bf16[32,2,11776]{2,1,0:T(2,128)(2,1)}, u32[]{:S(2)}, u32[]{:S(2)}) async-start(bf16[32,2,11776]{2,1,0:T(2,128)(2,1)} %reshape.102), calls=%async_computation.1 | async-start | bytes 3014656 | tf_op jit(solution)/shard_map/all_to_all | solution.py:73
  274.3 12.7 %copy-start.1 = (pred[256,2048]{1,0:T(8,128)(4,1)S(1)}, pred[256,2048]{1,0:T(8,128)(4,1)}, u32[]{:S(2)}) copy-start(pred[256,2048]{1,0:T(8,128)(4,1)} %fusion.4) | copy-start | bytes 1572868
Sparse Core Ops, SparseCore 0:
  9.2 102.9 all-gather.1
where the time goes:
time: 306 us; the launch traced here: 304 us
  blocking collectives  111 us (36%)
  local copies, waits for them, and re-layouts  87.4 us (29%)
  waiting for transfers between devices  60.9 us (20%)
  between operations  13.6 us (4%)
  matrix products  12 us (4%)
  starting transfers between devices  9.61 us (3%)
  other arithmetic  9.49 us (3%)
    all_to_all x1, blocking collectives, per_device(): lax.all_to_all(regrouped, 'beam', split_axis=0, concat_axis=1, tiled=True)  111 us
    all_to_all x1, waiting for transfers between devices, per_device(): lax.all_to_all(extended, 'beam', split_axis=0, concat_axis=2, tiled=True)  34.9 us
    reshape x2, local copies, waits for them, and re-layouts, per_device(): spectra.reshape(local_channels, frames, 2, subband_total, sub_width)  27.4 us
    ppermute x1, waiting for transfers between devices, from_behind(): return lax.ppermute(block, axis, route)  26 us
    unnamed x16, local copies, waits for them, and re-layouts  14.6 us
    reshape x1, local copies, waits for them, and re-layouts, per_device(): jnp.transpose(regrouped, (3, 0, 1, 2, 4))  14.2 us
    all_gather x1, local copies, waits for them, and re-layouts, per_device(): lax.all_gather(templates, 'beam', axis=2, tiled=True)  12.6 us
    all_to_all x2, local copies, waits for them, and re-layouts, per_device(): lax.all_to_all(extended, 'beam', split_axis=0, concat_axis=2, tiled=True)  8.12 us
  transfers between devices with their start and end apart: 3, of which 2 were waited for; matrix products, arithmetic and copies ran while one was open for 28% of the time, Pallas kernels for 0%

commit v1 on v0

v1 whole, which is shorter than its diff:
```python
import jax
import jax.numpy as jnp
from jax import lax
from jax.experimental import pallas as pl
from jax.experimental.pallas import tpu as pltpu
from jax.sharding import PartitionSpec as P

MESH = pl.DeviceIdType.MESH
CHUNKS = 4
LAGS = 8
F32 = jnp.float32
BF16 = jnp.bfloat16


def kernel(
    spec, steer, tmpl, tlen, bst, bwd, out,
    xbuf, wst, wmix, ppow, pin, tbuf, acc, sbuf, hsend, hrecv,
    w_own, w_send, w_recv, x_own, x_send, x_recv, t_send, t_recv, t2_send, t2_recv,
    p_own, p_send, p_recv, s_send, s_recv, h_send, h_recv,
):
    me = lax.axis_index("beam")
    tm = lax.axis_index("tm")
    core = me % 2
    sib = me + 1 - 2 * core
    chip = me // 2
    half = me // 16
    local = me % 16
    kk = local // 2
    partner = (me + 16) % 32

    def remote(src, dst, send_sem, recv_sem, beam, tm_index=None):
        return pltpu.make_async_remote_copy(
            src_ref=src, dst_ref=dst, send_sem=send_sem, recv_sem=recv_sem,
            device_id=(beam, tm if tm_index is None else tm_index), device_id_type=MESH,
        )

    def tile(device):
        return pl.ds(pl.multiple_of((device // 2) * 128, 128), 128)

    own_w = pltpu.make_async_copy(steer.at[0], wst.at[core], w_own)
    own_w.start()

    def own_x(g, _):
        pltpu.make_async_copy(
            spec.at[:, 4 * (g // 2) + 2 * core + g % 2, :, tile(me)],
            xbuf.at[g, pl.ds(32 * me, 32)], x_own,
        ).start()
        return 0

    lax.fori_loop(0, 8, own_x, 0)

    bins = 64 * me + lax.broadcasted_iota(jnp.int32, (64, 256), 0)
    first = bst[...]
    keep = jnp.where((bins >= first) & (bins < first + bwd[...]), 1, 0)
    length = jnp.broadcast_to(tlen[...], (64, 256))
    for lag in range(LAGS):
        tbuf[lag, kk, core] = jnp.where(
            (keep == 1) & (length > lag), tmpl[lag].astype(F32), 0.0
        ).astype(BF16)

    barrier = pltpu.get_barrier_semaphore()

    def greet(off, _):
        pl.semaphore_signal(barrier, inc=1, device_id=((me + off) % 32, tm), device_id_type=MESH)
        return 0

    lax.fori_loop(1, 32, greet, 0)
    for d in (1, 7):
        pl.semaphore_signal(barrier, inc=1, device_id=(me, (tm + d) % 8), device_id_type=MESH)
    pl.semaphore_wait(barrier, 33)

    w_copy = remote(steer.at[0], wst.at[core], w_send, w_recv, sib)
    w_copy.start()

    def send_x(j):
        def body(off, _):
            peer = (me + off) % 32
            for i in range(2):
                remote(
                    spec.at[:, 4 * j + 2 * (peer % 2) + i, :, tile(peer)],
                    xbuf.at[2 * j + i, pl.ds(32 * me, 32)],
                    x_send.at[j], x_recv.at[j], peer,
                ).start()
            return 0

        lax.fori_loop(1, 32, body, 0)

    send_x(0)

    def send_t(off, _):
        peer = 16 * half + (local + 2 * off) % 16
        remote(
            tbuf.at[:, kk, core], tbuf.at[:, kk, core], t_send, t_recv, peer
        ).start()
        return 0

    lax.fori_loop(1, 8, send_t, 0)
    send_x(1)

    own_w.wait()
    w_copy.wait_recv()
    row = lax.broadcasted_iota(jnp.int32, (256, 256), 0)
    col = lax.broadcasted_iota(jnp.int32, (256, 256), 1)
    e_even = jnp.where((row < 128) & (col == 2 * row), 1.0, 0.0)
    odd = (row >= 128) & (col == 2 * (row - 128) + 1)
    e_real = (e_even - jnp.where(odd, 1.0, 0.0)).astype(BF16)
    i_even = (row >= 128) & (col == 2 * (row - 128))
    i_odd = (row < 128) & (col == 2 * row + 1)
    e_imag = jnp.where(i_even | i_odd, 1.0, 0.0).astype(BF16)

    def mix(n, _):
        s, cb = n // 8, n % 8
        cols = pl.ds(pl.multiple_of(cb * 128, 128), 128)
        both = jnp.concatenate([wst[s, 0, :, cols], wst[s, 1, :, cols]], axis=1)
        outcols = pl.ds(pl.multiple_of(cb * 256, 256), 256)
        for ri, e in enumerate((e_real, e_imag)):
            m = jnp.dot(both, e, preferred_element_type=F32).astype(BF16)
            rows = pl.ds(pl.multiple_of((s * 2 + ri) * 128, 128), 128)
            wmix[:, rows, outcols] = m.reshape(4, 128, 256)
        return 0

    lax.fori_loop(0, 16, mix, 0)
    acc[...] = jnp.zeros_like(acc)

    xflat = xbuf.reshape(8, 2048, 128)
    lane = lax.broadcasted_iota(jnp.int32, (128, 256), 1)
    low = lane % 128 < 64

    def power(j):
        pltpu.make_async_copy(
            xbuf.at[pl.ds(0, 2), pl.ds(0, 992)], xbuf.at[pl.ds(0, 2), pl.ds(0, 992)], x_recv.at[j]
        ).wait()

        def block(b, _):
            x = jnp.concatenate([xflat[2 * j], xflat[2 * j + 1]], axis=1)
            y = jnp.dot(wmix[b], x, preferred_element_type=F32)
            ar, ai, br, bi = y[0:128], y[128:256], y[256:384], y[384:512]
            p = jnp.where(low, ar * ar + ai * ai, br * br + bi * bi).astype(BF16)
            for f in range(2):
                ppow[j, f, b // 2, b % 2] = p[:, f * 128 : (f + 1) * 128].reshape(8, 16, 128)
            return 0

        lax.fori_loop(0, 4, block, 0)

        pltpu.make_async_copy(
            ppow.at[j, :, :, local // 8, local % 8], pin.at[j, core, :, :, kk], p_own.at[j]
        ).start()

        def send_p(off, _):
            q = (local + off) % 16
            remote(
                ppow.at[j, :, :, q // 8, q % 8], pin.at[j, core, :, :, kk],
                p_send.at[j], p_recv.at[j], 16 * half + q,
            ).start()
            return 0

        lax.fori_loop(1, 16, send_p, 0)

    def seg(j):
        return (4 * j, 4) if j < CHUNKS - 1 else (12, 11)

    def score_copy(j):
        t0, n = seg(j)
        return remote(
            acc.at[pl.ds(t0, n), 1 - half], sbuf.at[pl.ds(t0, n)], s_send.at[j], s_recv.at[j], partner
        )

    def correlate(j):
        pltpu.make_async_copy(
            ppow.at[j, :, :, local // 8, local % 8], pin.at[j, core, :, :, kk], p_own.at[j]
        ).wait()
        wait_p(j)

        def lag_step(lag, _):
            parts = [pin[j, :, :, :, k].reshape(128, 128) for k in range(8)]
            lhs = jnp.concatenate(parts, axis=1)
            w = tbuf[lag].reshape(1024, 256)
            res = jnp.dot(lhs, w, preferred_element_type=F32).reshape(4, 2, 16, 256)
            rows = pl.ds(4 * j + 7 - lag, 4)
            acc[rows] = acc[rows] + res
            return 0

        lax.fori_loop(0, LAGS, lag_step, 0)
        score_copy(j).start()

    def wait_p(j):
        d = xbuf.at[0, pl.ds(0, 480)]
        pltpu.make_async_copy(d, d, p_recv.at[j]).wait()

    d = xbuf.at[pl.ds(0, 8), pl.ds(0, 32)]
    pltpu.make_async_copy(d, d, x_own).wait()
    power(0)
    send_x(2)
    d = tbuf.at[:, pl.ds(0, 7), 0]
    pltpu.make_async_copy(d, d, t_recv).wait()
    t2 = remote(tbuf.at[:, :, core], tbuf.at[:, :, core], t2_send, t2_recv, sib)
    t2.start()
    power(1)
    send_x(3)
    t2.wait_recv()
    correlate(0)
    power(2)
    correlate(1)
    power(3)
    correlate(2)

    score_copy(0).wait_recv()
    score_copy(1).wait_recv()
    h_copy = remote(hsend, hrecv, h_send, h_recv, me, (tm + 7) % 8)

    @pl.when(tm > 0)
    def _():
        hsend[...] = acc[0:7, half] + sbuf[0:7]
        h_copy.start()

    correlate(3)
    score_copy(2).wait_recv()
    score_copy(3).wait_recv()
    out[...] = acc[7:23, half] + sbuf[7:23]

    @pl.when(tm < 7)
    def _():
        h_copy.wait_recv()
        out[9:16] = out[9:16] + hrecv[...]

    w_copy.wait_send()
    t2.wait_send()
    d = tbuf.at[:, pl.ds(0, 7), 0]
    pltpu.make_async_copy(d, d, t_send).wait()
    for j in range(CHUNKS):
        d = xbuf.at[pl.ds(0, 2), pl.ds(0, 992)]
        pltpu.make_async_copy(d, d, x_send.at[j]).wait()
        d = xbuf.at[0, pl.ds(0, 480)]
        pltpu.make_async_copy(d, d, p_send.at[j]).wait()
        score_copy(j).wait_send()

    @pl.when(tm > 0)
    def _():
        h_copy.wait_send()


def per_device(spectra, steering, templates, tmpl_length, band_start, band_width):
    rows = [a.reshape(1, -1) for a in (tmpl_length, band_start, band_width)]
    by_bin = jnp.transpose(templates, (1, 2, 0))
    any_spec = pl.BlockSpec(memory_space=pl.ANY)
    vmem = pl.BlockSpec(memory_space=pltpu.VMEM)
    dma = pltpu.SemaphoreType.DMA
    scores = pl.pallas_call(
        kernel,
        out_shape=jax.ShapeDtypeStruct((16, 16, 256), F32),
        in_specs=[any_spec, any_spec, vmem, vmem, vmem, vmem],
        out_specs=vmem,
        scratch_shapes=[
            pltpu.VMEM((8, 1024, 2, 128), BF16),
            pltpu.VMEM((2, 2, 512, 1024), BF16),
            pltpu.VMEM((4, 512, 2048), BF16),
            pltpu.VMEM((4, 2, 2, 2, 8, 16, 128), BF16),
            pltpu.VMEM((4, 2, 2, 2, 8, 16, 128), BF16),
            pltpu.VMEM((8, 8, 2, 64, 256), BF16),
            pltpu.VMEM((23, 2, 16, 256), F32),
            pltpu.VMEM((23, 16, 256), F32),
            pltpu.VMEM((7, 16, 256), F32),
            pltpu.VMEM((7, 16, 256), F32),
            dma(()), dma(()), dma(()),
            dma(()), dma((4,)), dma((4,)),
            dma(()), dma(()), dma(()), dma(()),
            dma((4,)), dma((4,)), dma((4,)),
            dma((4,)), dma((4,)), dma(()), dma(()),
        ],
        compiler_params=pltpu.CompilerParams(
            collective_id=0, has_side_effects=True, vmem_limit_bytes=56 * 1024 * 1024
        ),
    )(spectra, steering, by_bin, *rows)
    return jnp.transpose(scores, (1, 0, 2))


def solution(mesh):
    return jax.shard_map(
        per_device,
        mesh=mesh,
        in_specs=(
            P("beam", "tm", None, None),
            P("beam", None, None, None),
            P(None, None, "beam"),
            P(),
            P(),
            P(),
        ),
        out_specs=P("beam", "tm", None),
        check_vma=False,
    )
```

time: 306 us -> 148 us (0.48)
  the two profiles are of different devices: /device:TPU:57 before, /device:TPU:1 now
where the time goes in v1:
time: 148 us
  Pallas kernels  146 us (99%)
  local copies, waits for them, and re-layouts  1.81 us (1%)
    pallas_call x1, Pallas kernels, per_device(): pl.pallas_call(kernel, out_shape=jax.ShapeDtypeStruct((16, 16, 256), F32)...  146 us

profile of v1, /device:TPU:1, one launch (start us, length us, event | category | flops | bytes accessed | tf_op | source)
XLA Modules:
  0.0 148.1 jit_solution(5371104589742184447)
XLA Ops:
  0.0 146.3 %shard_map.64 = f32[16,16,256]{2,1,0:T(8,128)} custom-call(bf16[32,16,2,2048]{3,2,1,0:T(2,128)(2,1)} %spec.1, bf16[1,2,512,1024]{3,2,1,0:T(8,128)(2,1)} %steer.1, bf16[8,64,256]{2,1,0:T(8,128)(2,1)} %bitcast.6, s32[1,256]{1,0:T(1,128)} %bitcast.7, s32[1,256]{1,0:T(1,128)} %bitcast.8, s32[1,256]{1,0:T(1,128)} %bitcast.9), custom_call_target="tpu_custom_call" | custom-call | tf_op jit(solution)/shard_map/pallas_call | solution.py:248
  146.3 1.8 %copy.7 = f32[16,16,256]{2,1,0:T(8,128)} copy(f32[16,16,256]{2,0,1:T(8,128)} %bitcast.5) | data formatting | bytes 524288 | tf_op jit(solution)/shard_map/transpose | solution.py:274

commit v2 on v1

v2 whole, which is shorter than its diff:
```python
import jax
import jax.numpy as jnp
from jax import lax
from jax.experimental import pallas as pl
from jax.experimental.pallas import tpu as pltpu
from jax.sharding import PartitionSpec as P

MESH = pl.DeviceIdType.MESH
CHUNKS = 8
LAGS = 8
SEGMENTS = ((0, 8), (8, 6), (14, 9))
F32 = jnp.float32
BF16 = jnp.bfloat16
SENT = BF16


def kernel(
    spec, steer, tmpl, tlen, bst, bwd, out,
    xbuf, wst, wmix, ppow, pin, tbuf, acc, ssend, sbuf, hsend, hrecv,
    w_own, w_send, w_recv, x_own, x_send, x_recv, t_send, t_recv, y_send, y_recv, t2_send, t2_recv,
    p_own, p_send, p_recv, s_send, s_recv, h_send, h_recv,
):
    me = lax.axis_index("beam")
    tm = lax.axis_index("tm")
    core = me % 2
    sib = me + 1 - 2 * core
    half = me // 16
    local = me % 16
    kk = local // 2
    partner = (me + 16) % 32
    quarter = tm % 4

    def remote(src, dst, send_sem, recv_sem, beam, tm_index=None):
        return pltpu.make_async_remote_copy(
            src_ref=src, dst_ref=dst, send_sem=send_sem, recv_sem=recv_sem,
            device_id=(beam, tm if tm_index is None else tm_index), device_id_type=MESH,
        )

    def y_peer(off):
        return tm - quarter + (quarter + off) % 4

    def wait_bytes(ref, sem):
        pltpu.make_async_copy(ref, ref, sem).wait()

    def tile(device):
        return pl.ds(pl.multiple_of((device // 2) * 128, 128), 128)

    barrier = pltpu.get_barrier_semaphore()

    def greet(off, _):
        pl.semaphore_signal(barrier, inc=1, device_id=((me + off) % 32, tm), device_id_type=MESH)
        return 0

    lax.fori_loop(1, 32, greet, 0)
    for off in (1, 2, 3):
        pl.semaphore_signal(barrier, inc=1, device_id=(me, y_peer(off)), device_id_type=MESH)

    @pl.when((tm == 3) | (tm == 4))
    def _():
        pl.semaphore_signal(barrier, inc=1, device_id=(me, 7 - tm), device_id_type=MESH)

    own_w = pltpu.make_async_copy(steer.at[0], wst.at[core], w_own)
    own_w.start()

    def own_x(j, _):
        pltpu.make_async_copy(
            spec.at[:, 2 * j + core, :, tile(me)], xbuf.at[j, pl.ds(32 * me, 32)], x_own
        ).start()
        return 0

    lax.fori_loop(0, CHUNKS, own_x, 0)

    bins = 64 * me + lax.broadcasted_iota(jnp.int32, (64, 256), 0)
    first = bst[...]
    keep = jnp.where((bins >= first) & (bins < first + bwd[...]), 1, 0)
    length = jnp.broadcast_to(tlen[...], (64, 256))
    for i in range(2):
        lag = 2 * quarter + i
        tbuf[lag, kk, core] = jnp.where(
            (keep == 1) & (length > lag), tmpl[lag].astype(F32), 0.0
        ).astype(BF16)

    pl.semaphore_wait(barrier, 34 + jnp.where((tm == 3) | (tm == 4), 1, 0))

    w_copy = remote(steer.at[0], wst.at[core], w_send, w_recv, sib)
    w_copy.start()

    def send_t(off, _):
        part = tbuf.at[pl.ds(2 * quarter, 2), kk, core]
        remote(part, part, t_send, t_recv, 16 * half + (local + 2 * off) % 16).start()
        return 0

    lax.fori_loop(1, 8, send_t, 0)

    def send_x(j):
        def body(off, _):
            peer = (me + off) % 32
            remote(
                spec.at[:, 2 * j + peer % 2, :, tile(peer)],
                xbuf.at[j, pl.ds(32 * me, 32)],
                x_send.at[j], x_recv.at[j], peer,
            ).start()
            return 0

        lax.fori_loop(1, 32, body, 0)

    send_x(0)
    send_x(1)

    own_w.wait()
    w_copy.wait_recv()
    row = lax.broadcasted_iota(jnp.int32, (256, 256), 0)
    col = lax.broadcasted_iota(jnp.int32, (256, 256), 1)
    e_even = jnp.where((row < 128) & (col == 2 * row), 1.0, 0.0)
    odd = (row >= 128) & (col == 2 * (row - 128) + 1)
    e_real = (e_even - jnp.where(odd, 1.0, 0.0)).astype(BF16)
    i_even = (row >= 128) & (col == 2 * (row - 128))
    i_odd = (row < 128) & (col == 2 * row + 1)
    e_imag = jnp.where(i_even | i_odd, 1.0, 0.0).astype(BF16)

    def mix(n, _):
        s, cb = n // 8, n % 8
        cols = pl.ds(pl.multiple_of(cb * 128, 128), 128)
        both = jnp.concatenate([wst[s, 0, :, cols], wst[s, 1, :, cols]], axis=1)
        outcols = pl.ds(pl.multiple_of(cb * 256, 256), 256)
        for ri, e in enumerate((e_real, e_imag)):
            m = jnp.dot(both, e, preferred_element_type=F32).astype(BF16)
            rows = pl.ds(pl.multiple_of((s * 2 + ri) * 128, 128), 128)
            wmix[:, rows, outcols] = m.reshape(4, 128, 256)
        return 0

    lax.fori_loop(0, 16, mix, 0)
    acc[...] = jnp.zeros_like(acc)

    wait_bytes(tbuf.at[pl.ds(0, 2), pl.ds(0, 7), 0], t_recv)
    for off in (1, 2, 3):
        part = tbuf.at[pl.ds(2 * quarter, 2), :, core]
        remote(part, part, y_send, y_recv, me, y_peer(off)).start()

    xflat = xbuf.reshape(CHUNKS, 2048, 128)
    low = lax.broadcasted_iota(jnp.int32, (128, 128), 1) < 64

    def own_p(j):
        return pltpu.make_async_copy(
            ppow.at[j, :, local // 8, local % 8], pin.at[j, core, :, kk], p_own.at[j]
        )

    def power(j):
        wait_bytes(xbuf.at[0, pl.ds(0, 992)], x_recv.at[j])

        def block(b, _):
            y = jnp.dot(wmix[b], xflat[j], preferred_element_type=F32)
            ar, ai, br, bi = y[0:128], y[128:256], y[256:384], y[384:512]
            p = jnp.where(low, ar * ar + ai * ai, br * br + bi * bi).astype(BF16)
            ppow[j, b // 2, b % 2] = p.reshape(8, 16, 128)
            return 0

        lax.fori_loop(0, 4, block, 0)
        own_p(j).start()

        def send_p(off, _):
            q = (local + off) % 16
            remote(
                ppow.at[j, :, q // 8, q % 8], pin.at[j, core, :, kk],
                p_send.at[j], p_recv.at[j], 16 * half + q,
            ).start()
            return 0

        lax.fori_loop(1, 16, send_p, 0)

    def correlate(j):
        own_p(j).wait()
        wait_bytes(xbuf.at[0, pl.ds(0, 240)], p_recv.at[j])

        def lag_step(lag, _):
            parts = [pin[j, :, :, k].reshape(64, 128) for k in range(8)]
            lhs = jnp.concatenate(parts, axis=1)
            w = tbuf[lag].reshape(1024, 256)
            res = jnp.dot(lhs, w, preferred_element_type=F32).reshape(2, 2, 16, 256)
            rows = pl.ds(2 * j + 7 - lag, 2)
            acc[rows] = acc[rows] + res
            return 0

        lax.fori_loop(0, LAGS, lag_step, 0)

    def score_copy(g):
        rows = pl.ds(*SEGMENTS[g])
        return remote(ssend.at[rows], sbuf.at[rows], s_send.at[g], s_recv.at[g], partner)

    def send_scores(g):
        rows = pl.ds(*SEGMENTS[g])
        ssend[rows] = acc[rows, 1 - half].astype(SENT)
        score_copy(g).start()

    t2 = remote(tbuf.at[:, :, core], tbuf.at[:, :, core], t2_send, t2_recv, sib)
    h_copy = remote(hsend, hrecv, h_send, h_recv, me, tm - 1)

    wait_bytes(xbuf.at[pl.ds(0, CHUNKS), pl.ds(0, 32)], x_own)
    power(0)
    send_x(2)
    power(1)
    send_x(3)
    power(2)
    send_x(4)
    wait_bytes(tbuf.at[pl.ds(0, 6), :, 0], y_recv)
    t2.start()
    power(3)
    send_x(5)
    t2.wait_recv()
    correlate(0)
    correlate(1)
    power(4)
    send_x(6)
    correlate(2)
    correlate(3)
    send_scores(0)
    power(5)
    send_x(7)
    correlate(4)
    power(6)
    correlate(5)

    score_copy(0).wait_recv()

    @pl.when(tm > 0)
    def _():
        hsend[...] = (acc[0:7, half] + sbuf[0:7].astype(F32)).astype(SENT)
        h_copy.start()

    power(7)
    correlate(6)
    send_scores(1)
    correlate(7)
    send_scores(2)
    score_copy(1).wait_recv()
    score_copy(2).wait_recv()
    out[...] = acc[7:23, half] + sbuf[7:23].astype(F32)

    @pl.when(tm < 7)
    def _():
        h_copy.wait_recv()
        out[9:16] = out[9:16] + hrecv[...].astype(F32)

    w_copy.wait_send()
    t2.wait_send()
    wait_bytes(tbuf.at[pl.ds(0, 2), pl.ds(0, 7), 0], t_send)
    wait_bytes(tbuf.at[pl.ds(0, 6), :, 0], y_send)
    for j in range(CHUNKS):
        wait_bytes(xbuf.at[0, pl.ds(0, 992)], x_send.at[j])
        wait_bytes(xbuf.at[0, pl.ds(0, 240)], p_send.at[j])
    for g in range(3):
        score_copy(g).wait_send()

    @pl.when(tm > 0)
    def _():
        h_copy.wait_send()


def per_device(spectra, steering, templates, tmpl_length, band_start, band_width):
    rows = [a.reshape(1, -1) for a in (tmpl_length, band_start, band_width)]
    by_bin = jnp.transpose(templates, (1, 2, 0))
    any_spec = pl.BlockSpec(memory_space=pl.ANY)
    vmem = pl.BlockSpec(memory_space=pltpu.VMEM)
    dma = pltpu.SemaphoreType.DMA
    scores = pl.pallas_call(
        kernel,
        out_shape=jax.ShapeDtypeStruct((16, 16, 256), F32),
        in_specs=[any_spec, any_spec, vmem, vmem, vmem, vmem],
        out_specs=vmem,
        scratch_shapes=[
            pltpu.VMEM((8, 1024, 2, 128), BF16),
            pltpu.VMEM((2, 2, 512, 1024), BF16),
            pltpu.VMEM((4, 512, 2048), BF16),
            pltpu.VMEM((8, 2, 2, 8, 16, 128), BF16),
            pltpu.VMEM((8, 2, 2, 8, 16, 128), BF16),
            pltpu.VMEM((8, 8, 2, 64, 256), BF16),
            pltpu.VMEM((23, 2, 16, 256), F32),
            pltpu.VMEM((23, 16, 256), SENT),
            pltpu.VMEM((23, 16, 256), SENT),
            pltpu.VMEM((7, 16, 256), SENT),
            pltpu.VMEM((7, 16, 256), SENT),
            dma(()), dma(()), dma(()),
            dma(()), dma((8,)), dma((8,)),
            dma(()), dma(()), dma(()), dma(()), dma(()), dma(()),
            dma((8,)), dma((8,)), dma((8,)),
            dma((3,)), dma((3,)), dma(()), dma(()),
        ],
        compiler_params=pltpu.CompilerParams(
            collective_id=0, has_side_effects=True, vmem_limit_bytes=56 * 1024 * 1024
        ),
    )(spectra, steering, by_bin, *rows)
    return jnp.transpose(scores, (1, 0, 2))


def solution(mesh):
    return jax.shard_map(
        per_device,
        mesh=mesh,
        in_specs=(
            P("beam", "tm", None, None),
            P("beam", None, None, None),
            P(None, None, "beam"),
            P(),
            P(),
            P(),
        ),
        out_specs=P("beam", "tm", None),
        check_vma=False,
    )
```

time: 148 us -> 125 us (0.84)
  Pallas kernels: 146 us -> 122 us
    pallas_call x1, Pallas kernels: 146 us -> 122 us  [per_device(): pl.pallas_call(kernel, out_shape=jax.ShapeDtypeStruct((16, 16, 256), F32)...]
where the time goes in v2:
time: 125 us; the launch traced here: 124 us
  Pallas kernels  122 us (98%)
  local copies, waits for them, and re-layouts  1.81 us (1%)
    pallas_call x1, Pallas kernels, per_device(): pl.pallas_call(kernel, out_shape=jax.ShapeDtypeStruct((16, 16, 256), F32)...  122 us

profile of v2, /device:TPU:1, one launch (start us, length us, event | category | flops | bytes accessed | tf_op | source)
XLA Modules:
  0.0 123.9 jit_solution(4830538348994557719)
XLA Ops:
  0.0 122.1 %shard_map.64 = f32[16,16,256]{2,1,0:T(8,128)} custom-call(bf16[32,16,2,2048]{3,2,1,0:T(2,128)(2,1)} %spec.1, bf16[1,2,512,1024]{3,2,1,0:T(8,128)(2,1)} %steer.1, bf16[8,64,256]{2,1,0:T(8,128)(2,1)} %bitcast.6, s32[1,256]{1,0:T(1,128)} %bitcast.7, s32[1,256]{1,0:T(1,128)} %bitcast.8, s32[1,256]{1,0:T(1,128)} %bitcast.9), custom_call_target="tpu_custom_call" | custom-call | tf_op jit(solution)/shard_map/pallas_call | solution.py:265
  122.1 1.8 %copy.7 = f32[16,16,256]{2,1,0:T(8,128)} copy(f32[16,16,256]{2,0,1:T(8,128)} %bitcast.5) | data formatting | bytes 524288 | tf_op jit(solution)/shard_map/transpose | solution.py:292

commit v3 on v2

--- a/solution.py
+++ b/solution.py
@@ -8,7 +8,7 @@
 MESH = pl.DeviceIdType.MESH
 CHUNKS = 8
 LAGS = 8
-SEGMENTS = ((0, 8), (8, 6), (14, 9))
+SEGMENTS = ((0, 8), (8, 6), (14, 4), (18, 5))
 F32 = jnp.float32
 BF16 = jnp.bfloat16
 SENT = BF16
@@ -16,6 +16,7 @@
 
 def kernel(
     spec, steer, tmpl, tlen, bst, bwd, out,
+    tmpl_v, rows_v, m_own,
     xbuf, wst, wmix, ppow, pin, tbuf, acc, ssend, sbuf, hsend, hrecv,
     w_own, w_send, w_recv, x_own, x_send, x_recv, t_send, t_recv, y_send, y_recv, t2_send, t2_recv,
     p_own, p_send, p_recv, s_send, s_recv, h_send, h_recv,
@@ -61,6 +62,14 @@
 
     own_w = pltpu.make_async_copy(steer.at[0], wst.at[core], w_own)
     own_w.start()
+    own_t = pltpu.make_async_copy(tmpl.at[pl.ds(2 * quarter, 2)], tmpl_v, m_own.at[0])
+    own_t.start()
+    own_r = [
+        pltpu.make_async_copy(a, rows_v.at[i], m_own.at[1 + i])
+        for i, a in enumerate((tlen, bst, bwd))
+    ]
+    for c in own_r:
+        c.start()
 
     def own_x(j, _):
         pltpu.make_async_copy(
@@ -71,13 +80,16 @@
     lax.fori_loop(0, CHUNKS, own_x, 0)
 
     bins = 64 * me + lax.broadcasted_iota(jnp.int32, (64, 256), 0)
-    first = bst[...]
-    keep = jnp.where((bins >= first) & (bins < first + bwd[...]), 1, 0)
-    length = jnp.broadcast_to(tlen[...], (64, 256))
+    own_t.wait()
+    for c in own_r:
+        c.wait()
+    first = rows_v[1]
+    keep = jnp.where((bins >= first) & (bins < first + rows_v[2]), 1, 0)
+    length = jnp.broadcast_to(rows_v[0], (64, 256))
     for i in range(2):
         lag = 2 * quarter + i
         tbuf[lag, kk, core] = jnp.where(
-            (keep == 1) & (length > lag), tmpl[lag].astype(F32), 0.0
+            (keep == 1) & (length > lag), tmpl_v[i].astype(F32), 0.0
         ).astype(BF16)
 
     pl.semaphore_wait(barrier, 34 + jnp.where((tm == 3) | (tm == 4), 1, 0))
@@ -90,11 +102,10 @@
         remote(part, part, t_send, t_recv, 16 * half + (local + 2 * off) % 16).start()
         return 0
 
-    lax.fori_loop(1, 8, send_t, 0)
 
     def send_x(j):
         def body(off, _):
-            peer = (me + off) % 32
+            peer = (16 * (1 - half) + (local + off) % 16 + 16 * (off // 16)) % 32
             remote(
                 spec.at[:, 2 * j + peer % 2, :, tile(peer)],
                 xbuf.at[j, pl.ds(32 * me, 32)],
@@ -102,10 +113,13 @@
             ).start()
             return 0
 
-        lax.fori_loop(1, 32, body, 0)
+        lax.fori_loop(0, 16, body, 0)
+        lax.fori_loop(17, 32, body, 0)
 
     send_x(0)
+    lax.fori_loop(1, 8, send_t, 0)
     send_x(1)
+    send_x(2)
 
     own_w.wait()
     w_copy.wait_recv()
@@ -148,31 +162,35 @@
     def power(j):
         wait_bytes(xbuf.at[0, pl.ds(0, 992)], x_recv.at[j])
 
-        def block(b, _):
+        def block(zh, zl):
+            b = 2 * zh + zl
             y = jnp.dot(wmix[b], xflat[j], preferred_element_type=F32)
             ar, ai, br, bi = y[0:128], y[128:256], y[256:384], y[384:512]
             p = jnp.where(low, ar * ar + ai * ai, br * br + bi * bi).astype(BF16)
-            ppow[j, b // 2, b % 2] = p.reshape(8, 16, 128)
-            return 0
-
-        lax.fori_loop(0, 4, block, 0)
-        own_p(j).start()
-
-        def send_p(off, _):
-            q = (local + off) % 16
+            ppow[j, zh, zl] = p.reshape(8, 16, 128)
+            return zl
+
+        def send_p(off, far):
+            q = 8 * ((local // 8 + far) % 2) + (local + off) % 8
             remote(
                 ppow.at[j, :, q // 8, q % 8], pin.at[j, core, :, kk],
                 p_send.at[j], p_recv.at[j], 16 * half + q,
             ).start()
-            return 0
-
-        lax.fori_loop(1, 16, send_p, 0)
-
-    def correlate(j):
+            return far
+
+        lax.fori_loop(0, 2, block, 1 - local // 8)
+        lax.fori_loop(0, 8, send_p, 1)
+        lax.fori_loop(0, 2, block, local // 8)
+        own_p(j).start()
+        lax.fori_loop(1, 8, send_p, 0)
+
+    def arrived(j):
         own_p(j).wait()
         wait_bytes(xbuf.at[0, pl.ds(0, 240)], p_recv.at[j])
 
-        def lag_step(lag, _):
+    def correlate(j, start=0, stop=LAGS):
+        def lag_step(step, _):
+            lag = LAGS - 1 - step
             parts = [pin[j, :, :, k].reshape(64, 128) for k in range(8)]
             lhs = jnp.concatenate(parts, axis=1)
             w = tbuf[lag].reshape(1024, 256)
@@ -181,7 +199,7 @@
             acc[rows] = acc[rows] + res
             return 0
 
-        lax.fori_loop(0, LAGS, lag_step, 0)
+        lax.fori_loop(start, stop, lag_step, 0)
 
     def score_copy(g):
         rows = pl.ds(*SEGMENTS[g])
@@ -197,27 +215,32 @@
 
     wait_bytes(xbuf.at[pl.ds(0, CHUNKS), pl.ds(0, 32)], x_own)
     power(0)
-    send_x(2)
+    send_x(3)
     power(1)
-    send_x(3)
+    send_x(4)
     power(2)
-    send_x(4)
+    send_x(5)
     wait_bytes(tbuf.at[pl.ds(0, 6), :, 0], y_recv)
     t2.start()
     power(3)
-    send_x(5)
+    send_x(6)
     t2.wait_recv()
+    arrived(0)
     correlate(0)
+    arrived(1)
     correlate(1)
     power(4)
-    send_x(6)
+    send_x(7)
+    arrived(2)
     correlate(2)
+    arrived(3)
     correlate(3)
     send_scores(0)
     power(5)
-    send_x(7)
+    arrived(4)
     correlate(4)
     power(6)
+    arrived(5)
     correlate(5)
 
     score_copy(0).wait_recv()
@@ -228,12 +251,17 @@
         h_copy.start()
 
     power(7)
+    arrived(6)
     correlate(6)
     send_scores(1)
-    correlate(7)
+    arrived(7)
+    correlate(7, 0, 4)
     send_scores(2)
+    correlate(7, 4, 8)
+    send_scores(3)
     score_copy(1).wait_recv()
     score_copy(2).wait_recv()
+    score_copy(3).wait_recv()
     out[...] = acc[7:23, half] + sbuf[7:23].astype(F32)
 
     @pl.when(tm < 7)
@@ -248,7 +276,7 @@
     for j in range(CHUNKS):
         wait_bytes(xbuf.at[0, pl.ds(0, 992)], x_send.at[j])
         wait_bytes(xbuf.at[0, pl.ds(0, 240)], p_send.at[j])
-    for g in range(3):
+    for g in range(4):
         score_copy(g).wait_send()
 
     @pl.when(tm > 0)
@@ -265,9 +293,12 @@
     scores = pl.pallas_call(
         kernel,
         out_shape=jax.ShapeDtypeStruct((16, 16, 256), F32),
-        in_specs=[any_spec, any_spec, vmem, vmem, vmem, vmem],
+        in_specs=[any_spec] * 6,
         out_specs=vmem,
         scratch_shapes=[
+            pltpu.VMEM((2, 64, 256), BF16),
+            pltpu.VMEM((3, 1, 256), jnp.int32),
+            dma((4,)),
             pltpu.VMEM((8, 1024, 2, 128), BF16),
             pltpu.VMEM((2, 2, 512, 1024), BF16),
             pltpu.VMEM((4, 512, 2048), BF16),
@@ -283,7 +314,7 @@
             dma(()), dma((8,)), dma((8,)),
             dma(()), dma(()), dma(()), dma(()), dma(()), dma(()),
             dma((8,)), dma((8,)), dma((8,)),
-            dma((3,)), dma((3,)), dma(()), dma(()),
+            dma((4,)), dma((4,)), dma(()), dma(()),
         ],
         compiler_params=pltpu.CompilerParams(
             collective_id=0, has_side_effects=True, vmem_limit_bytes=56 * 1024 * 1024

time: 125 us -> 119 us (0.952); the launches traced: 124 us -> 119 us
  Pallas kernels: 122 us -> 117 us
    pallas_call x1, Pallas kernels: 122 us -> 117 us  [per_device(): pl.pallas_call(kernel, out_shape=jax.ShapeDtypeStruct((16, 16, 256), F32)...]
where the time goes in v3:
time: 119 us
  Pallas kernels  117 us (98%)
  local copies, waits for them, and re-layouts  1.81 us (2%)
    pallas_call x1, Pallas kernels, per_device(): pl.pallas_call(kernel, out_shape=jax.ShapeDtypeStruct((16, 16, 256), F32)...  117 us

profile of v3, /device:TPU:1, one launch (start us, length us, event | category | flops | bytes accessed | tf_op | source)
XLA Modules:
  0.0 119.2 jit_solution(6518662962269835370)
XLA Ops:
  0.0 117.4 %shard_map.64 = f32[16,16,256]{2,1,0:T(8,128)} custom-call(bf16[32,16,2,2048]{3,2,1,0:T(2,128)(2,1)} %spec.1, bf16[1,2,512,1024]{3,2,1,0:T(8,128)(2,1)} %steer.1, bf16[8,64,256]{2,1,0:T(8,128)(2,1)} %bitcast.6, s32[1,256]{1,0:T(1,128)} %bitcast.7, s32[1,256]{1,0:T(1,128)} %bitcast.8, s32[1,256]{1,0:T(1,128)} %bitcast.9), custom_call_target="tpu_custom_call" | custom-call | tf_op jit(solution)/shard_map/pallas_call | solution.py:293
  117.4 1.8 %copy.7 = f32[16,16,256]{2,1,0:T(8,128)} copy(f32[16,16,256]{2,0,1:T(8,128)} %bitcast.5) | data formatting | bytes 524288 | tf_op jit(solution)/shard_map/transpose | solution.py:323

commit v4 on v3

--- a/solution.py
+++ b/solution.py
@@ -16,7 +16,7 @@
 
 def kernel(
     spec, steer, tmpl, tlen, bst, bwd, out,
-    tmpl_v, rows_v, m_own,
+    tmpl_v, rows_v, m_own, rounds, tell_sem,
     xbuf, wst, wmix, ppow, pin, tbuf, acc, ssend, sbuf, hsend, hrecv,
     w_own, w_send, w_recv, x_own, x_send, x_recv, t_send, t_recv, y_send, y_recv, t2_send, t2_recv,
     p_own, p_send, p_recv, s_send, s_recv, h_send, h_recv,
@@ -48,17 +48,41 @@
 
     barrier = pltpu.get_barrier_semaphore()
 
+    row = me // 8
+    sides = 2 - jnp.where((row == 0) | (row == 3), 1, 0)
+
+    def signal(sem, beam, tm_index):
+        pl.semaphore_signal(sem, inc=1, device_id=(beam, tm_index), device_id_type=MESH)
+
+    def greet_rows(sem):
+        @pl.when(row < 3)
+        def _():
+            signal(sem, me + 8, tm)
+
+        @pl.when(row > 0)
+        def _():
+            signal(sem, me - 8, tm)
+
+    greet_rows(barrier)
+
     def greet(off, _):
-        pl.semaphore_signal(barrier, inc=1, device_id=((me + off) % 32, tm), device_id_type=MESH)
+        signal(barrier, 8 * row + (me + off) % 8, tm)
         return 0
 
-    lax.fori_loop(1, 32, greet, 0)
+    lax.fori_loop(1, 8, greet, 0)
     for off in (1, 2, 3):
-        pl.semaphore_signal(barrier, inc=1, device_id=(me, y_peer(off)), device_id_type=MESH)
-
-    @pl.when((tm == 3) | (tm == 4))
-    def _():
-        pl.semaphore_signal(barrier, inc=1, device_id=(me, 7 - tm), device_id_type=MESH)
+        signal(barrier, me, y_peer(off))
+
+    teller = (tm == 0) & (row == 3)
+    told = (tm == 4) & (row == 0)
+
+    @pl.when(teller)
+    def _():
+        signal(barrier, me - 24, 4)
+
+    @pl.when(told)
+    def _():
+        signal(barrier, me + 24, 0)
 
     own_w = pltpu.make_async_copy(steer.at[0], wst.at[core], w_own)
     own_w.start()
@@ -92,7 +116,8 @@
             (keep == 1) & (length > lag), tmpl_v[i].astype(F32), 0.0
         ).astype(BF16)
 
-    pl.semaphore_wait(barrier, 34 + jnp.where((tm == 3) | (tm == 4), 1, 0))
+    pl.semaphore_wait(barrier, 10 + sides + jnp.where(teller | told, 1, 0))
+    greet_rows(rounds.at[0])
 
     w_copy = remote(steer.at[0], wst.at[core], w_send, w_recv, sib)
     w_copy.start()
@@ -102,6 +127,17 @@
         remote(part, part, t_send, t_recv, 16 * half + (local + 2 * off) % 16).start()
         return 0
 
+
+    def send_row(away, start):
+        def body(off, _):
+            peer = 8 * (row + away) + (me + off) % 8
+            remote(
+                spec.at[:, peer % 2, :, tile(peer)], xbuf.at[0, pl.ds(32 * me, 32)],
+                x_send.at[0], x_recv.at[0], peer,
+            ).start()
+            return 0
+
+        lax.fori_loop(start, 8, body, 0)
 
     def send_x(j):
         def body(off, _):
@@ -116,20 +152,33 @@
         lax.fori_loop(0, 16, body, 0)
         lax.fori_loop(17, 32, body, 0)
 
-    send_x(0)
+    send_row(0, 1)
+    for far in (1, 2, 3):
+        pl.semaphore_wait(rounds.at[far - 1], sides)
+        if far < 3:
+            greet_rows(rounds.at[far])
+
+        @pl.when(row + far < 4)
+        def _():
+            send_row(far, 0)
+
+        @pl.when(row >= far)
+        def _():
+            send_row(-far, 0)
+
     lax.fori_loop(1, 8, send_t, 0)
     send_x(1)
     send_x(2)
 
     own_w.wait()
     w_copy.wait_recv()
-    row = lax.broadcasted_iota(jnp.int32, (256, 256), 0)
+    line = lax.broadcasted_iota(jnp.int32, (256, 256), 0)
     col = lax.broadcasted_iota(jnp.int32, (256, 256), 1)
-    e_even = jnp.where((row < 128) & (col == 2 * row), 1.0, 0.0)
-    odd = (row >= 128) & (col == 2 * (row - 128) + 1)
+    e_even = jnp.where((line < 128) & (col == 2 * line), 1.0, 0.0)
+    odd = (line >= 128) & (col == 2 * (line - 128) + 1)
     e_real = (e_even - jnp.where(odd, 1.0, 0.0)).astype(BF16)
-    i_even = (row >= 128) & (col == 2 * (row - 128))
-    i_odd = (row < 128) & (col == 2 * row + 1)
+    i_even = (line >= 128) & (col == 2 * (line - 128))
+    i_odd = (line < 128) & (col == 2 * line + 1)
     e_imag = jnp.where(i_even | i_odd, 1.0, 0.0).astype(BF16)
 
     def mix(n, _):
@@ -215,6 +264,11 @@
 
     wait_bytes(xbuf.at[pl.ds(0, CHUNKS), pl.ds(0, 32)], x_own)
     power(0)
+
+    @pl.when(teller)
+    def _():
+        signal(tell_sem, me - 24, 4)
+
     send_x(3)
     power(1)
     send_x(4)
@@ -222,6 +276,10 @@
     send_x(5)
     wait_bytes(tbuf.at[pl.ds(0, 6), :, 0], y_recv)
     t2.start()
+    @pl.when(told)
+    def _():
+        pl.semaphore_wait(tell_sem, 1)
+
     power(3)
     send_x(6)
     t2.wait_recv()
@@ -243,6 +301,8 @@
     arrived(5)
     correlate(5)
 
+    power(7)
+
     score_copy(0).wait_recv()
 
     @pl.when(tm > 0)
@@ -250,7 +310,6 @@
         hsend[...] = (acc[0:7, half] + sbuf[0:7].astype(F32)).astype(SENT)
         h_copy.start()
 
-    power(7)
     arrived(6)
     correlate(6)
     send_scores(1)
@@ -299,6 +358,8 @@
             pltpu.VMEM((2, 64, 256), BF16),
             pltpu.VMEM((3, 1, 256), jnp.int32),
             dma((4,)),
+            pltpu.SemaphoreType.REGULAR((3,)),
+            pltpu.SemaphoreType.REGULAR,
             pltpu.VMEM((8, 1024, 2, 128), BF16),
             pltpu.VMEM((2, 2, 512, 1024), BF16),
             pltpu.VMEM((4, 512, 2048), BF16),

time: 119 us -> 119 us (level)
  no operation moved by 1% of the time
where the time goes in v4:
time: 119 us
  Pallas kernels  117 us (98%)
  local copies, waits for them, and re-layouts  1.81 us (2%)
    pallas_call x1, Pallas kernels, per_device(): pl.pallas_call(kernel, out_shape=jax.ShapeDtypeStruct((16, 16, 256), F32)...  117 us

profile of v4, /device:TPU:1, one launch (start us, length us, event | category | flops | bytes accessed | tf_op | source)
XLA Modules:
  0.0 118.5 jit_solution(14102325307322987186)
XLA Ops:
  0.0 116.7 %shard_map.64 = f32[16,16,256]{2,1,0:T(8,128)} custom-call(bf16[32,16,2,2048]{3,2,1,0:T(2,128)(2,1)} %spec.1, bf16[1,2,512,1024]{3,2,1,0:T(8,128)(2,1)} %steer.1, bf16[8,64,256]{2,1,0:T(8,128)(2,1)} %bitcast.6, s32[1,256]{1,0:T(1,128)} %bitcast.7, s32[1,256]{1,0:T(1,128)} %bitcast.8, s32[1,256]{1,0:T(1,128)} %bitcast.9), custom_call_target="tpu_custom_call" | custom-call | tf_op jit(solution)/shard_map/pallas_call | solution.py:352
  116.7 1.8 %copy.7 = f32[16,16,256]{2,1,0:T(8,128)} copy(f32[16,16,256]{2,0,1:T(8,128)} %bitcast.5) | data formatting | bytes 524288 | tf_op jit(solution)/shard_map/transpose | solution.py:384

commit v5 on v4

--- a/solution.py
+++ b/solution.py
@@ -227,9 +227,9 @@
             ).start()
             return far
 
-        lax.fori_loop(0, 2, block, 1 - local // 8)
+        lax.fori_loop(0, 2, block, 1 - local // 8, unroll=j >= 7)
         lax.fori_loop(0, 8, send_p, 1)
-        lax.fori_loop(0, 2, block, local // 8)
+        lax.fori_loop(0, 2, block, local // 8, unroll=j >= 7)
         own_p(j).start()
         lax.fori_loop(1, 8, send_p, 0)
 
@@ -248,7 +248,7 @@
             acc[rows] = acc[rows] + res
             return 0
 
-        lax.fori_loop(start, stop, lag_step, 0)
+        lax.fori_loop(start, stop, lag_step, 0, unroll=j >= 6)
 
     def score_copy(g):
         rows = pl.ds(*SEGMENTS[g])

time: 119 us -> 118 us (level)
  no operation moved by 1% of the time
where the time goes in v5:
time: 118 us
  Pallas kernels  116 us (98%)
  local copies, waits for them, and re-layouts  1.81 us (2%)
    pallas_call x1, Pallas kernels, per_device(): pl.pallas_call(kernel, out_shape=jax.ShapeDtypeStruct((16, 16, 256), F32)...  116 us

profile of v5, /device:TPU:1, one launch (start us, length us, event | category | flops | bytes accessed | tf_op | source)
XLA Modules:
  0.0 118.1 jit_solution(10881019206999234716)
XLA Ops:
  0.0 116.3 %shard_map.64 = f32[16,16,256]{2,1,0:T(8,128)} custom-call(bf16[32,16,2,2048]{3,2,1,0:T(2,128)(2,1)} %spec.1, bf16[1,2,512,1024]{3,2,1,0:T(8,128)(2,1)} %steer.1, bf16[8,64,256]{2,1,0:T(8,128)(2,1)} %bitcast.6, s32[1,256]{1,0:T(1,128)} %bitcast.7, s32[1,256]{1,0:T(1,128)} %bitcast.8, s32[1,256]{1,0:T(1,128)} %bitcast.9), custom_call_target="tpu_custom_call" | custom-call | tf_op jit(solution)/shard_map/pallas_call | solution.py:352
  116.3 1.8 %copy.7 = f32[16,16,256]{2,1,0:T(8,128)} copy(f32[16,16,256]{2,0,1:T(8,128)} %bitcast.5) | data formatting | bytes 524288 | tf_op jit(solution)/shard_map/transpose | solution.py:384
